TPU v7x, 32 devices: a whole 2x2x4 slice. The times are simulated.
32 devices in a mesh: tm: 8 (over y, x, core), strip: 4 (over z).
Axes of the slice: x: 2, y: 2, z: 4, core: 2. Of those that a mesh axis runs over, the one named last changes fastest.
Arguments:
- signal: bfloat16 [2, 16, 16384], P(None, 'strip', 'tm'), may hold values from -5 to 5
Outputs:
- spectrum: bfloat16 [2, 256, 16, 8, 2048], P(None, 'strip', None, 'tm')
All inputs are finite; a program needn't handle non-finite values.
Results may differ from a plain program's by a relative error of at most 0.0069.
Values may be sent and summed in bfloat16 or wider, within the bound.
A program may use at most 128 MiB of HBM per device.

v0:
```python
import math

import jax
import jax.numpy as jnp
from jax import lax
from jax.sharding import PartitionSpec as P

K = 256


TWO_PI = 2.0 * math.pi


def passed_along(value, axis, steps):
    count = lax.axis_size(axis)
    leading, last = (max(0, -steps), min(count, count - steps))
    return lax.ppermute(value, axis, [(source, source + steps) for source in range(leading, last)])


def channel_filters(channel_ids, length):
    offsets = jnp.arange(length, dtype=jnp.int32)
    phases = channel_ids[:, None] * offsets[None, :] % length
    angles = jnp.float32(TWO_PI) * phases.astype(jnp.float32) / length
    hamming = 0.54 - 0.46 * jnp.cos(jnp.float32(TWO_PI) * offsets.astype(jnp.float32) / length)
    scaled = hamming[None, :] / math.sqrt(length)
    cosine = scaled * jnp.cos(angles)
    sine = scaled * jnp.sin(angles)
    real_rows = jnp.stack([cosine, sine], axis=1)
    imag_rows = jnp.stack([-sine, cosine], axis=1)
    return jnp.concatenate([real_rows, imag_rows], axis=0).astype(jnp.bfloat16)


def dft_pair(first, second, modulus, norm):
    phases = first[:, None] * second[None, :] % modulus
    angles = jnp.float32(TWO_PI) * phases.astype(jnp.float32) / modulus
    return (jnp.cos(angles) * norm, jnp.sin(angles) * norm)


def channelize(extended, filters, channel_count, length):
    outcome = lax.conv_general_dilated(
        extended,
        filters,
        (1,),
        "VALID",
        dimension_numbers=("CNH", "OIH", "CNH"),
        preferred_element_type=jnp.float32,
    )
    window_count = extended.shape[1]
    spectra = outcome[:, :, :length].reshape(2, channel_count, window_count, length)
    centered = extended[:, :, K // 2 : K // 2 + length].astype(jnp.float32)
    real_part = spectra[0] * centered[0][None] + spectra[1] * centered[1][None]
    imag_part = spectra[1] * centered[0][None] - spectra[0] * centered[1][None]
    return jnp.stack([real_part, imag_part]).astype(jnp.bfloat16)


def first_pass(values):
    residues = lax.axis_size("tm")
    block_len = values.shape[2]
    piece_len = block_len // residues
    total_len = block_len * residues
    grouped = values.reshape(2, values.shape[1], residues, piece_len)
    res_ids = jnp.arange(residues, dtype=jnp.int32)
    small_cos, small_sin = dft_pair(res_ids, res_ids, residues, 1.0 / math.sqrt(residues))
    small_cos = small_cos.astype(jnp.bfloat16)
    small_sin = small_sin.astype(jnp.bfloat16)
    section_real = jnp.einsum(
        "qn,rns->rqs", small_cos, grouped[0], preferred_element_type=jnp.float32
    ) + jnp.einsum("qn,rns->rqs", small_sin, grouped[1], preferred_element_type=jnp.float32)
    section_imag = jnp.einsum(
        "qn,rns->rqs", small_cos, grouped[1], preferred_element_type=jnp.float32
    ) - jnp.einsum("qn,rns->rqs", small_sin, grouped[0], preferred_element_type=jnp.float32)
    sample_ids = lax.axis_index("tm") * piece_len + jnp.arange(piece_len, dtype=jnp.int32)
    twid_cos, twid_sin = dft_pair(res_ids, sample_ids, total_len, 1.0)
    turned_real = section_real * twid_cos[None] + section_imag * twid_sin[None]
    turned_imag = section_imag * twid_cos[None] - section_real * twid_sin[None]
    turned = jnp.stack([turned_real, turned_imag]).astype(jnp.bfloat16)
    return turned.reshape(2, values.shape[1], residues * piece_len)


def second_pass(values):
    block_len = values.shape[2]
    blk_ids = jnp.arange(block_len, dtype=jnp.int32)
    big_cos, big_sin = dft_pair(blk_ids, blk_ids, block_len, 1.0 / math.sqrt(block_len))
    big_cos = big_cos.astype(jnp.bfloat16)
    big_sin = big_sin.astype(jnp.bfloat16)
    out_real = jnp.dot(values[0], big_cos, preferred_element_type=jnp.float32) + jnp.dot(
        values[1], big_sin, preferred_element_type=jnp.float32
    )
    out_imag = jnp.dot(values[1], big_cos, preferred_element_type=jnp.float32) - jnp.dot(
        values[0], big_sin, preferred_element_type=jnp.float32
    )
    return jnp.stack([out_real, out_imag]).astype(jnp.bfloat16)


def per_device(signal):
    block_len = signal.shape[2]
    local_chan = K // lax.axis_size("strip")
    following = passed_along(signal[:, :, :K], "tm", -1)
    extended = jnp.concatenate([signal, following], axis=2)
    every_window = lax.all_gather(extended, "strip", axis=1, tiled=True)
    channel_ids = lax.axis_index("strip") * local_chan + jnp.arange(local_chan, dtype=jnp.int32)
    filters = channel_filters(channel_ids, K)
    products = channelize(every_window, filters, local_chan, block_len)
    window_total = products.shape[2]
    strips = products.reshape(2, local_chan * window_total, block_len)
    partial_sums = first_pass(lax.all_to_all(strips, "tm", split_axis=2, concat_axis=2, tiled=True))
    finished = second_pass(
        lax.all_to_all(partial_sums, "tm", split_axis=2, concat_axis=2, tiled=True)
    )
    return finished.reshape(2, local_chan, window_total, 1, block_len)


def solution(mesh):
    placed = (P(None, "strip", "tm"),)
    return jax.shard_map(
        per_device,
        mesh=mesh,
        in_specs=placed,
        out_specs=P(None, "strip", None, "tm", None),
        check_vma=False,
    )
```

profile of v0, /device:TPU:0, one launch (start us, length us, event | category | flops | bytes accessed | tf_op | source)
XLA Modules:
  0.0 851.7 jit_solution(14918469817403316897)
XLA Ops:
  4.6 15.4 %all_gather.3 = bf16[2,16,2304]{2,0,1:T(2,128)(2,1)S(1)} all-gather(bf16[2,4,2304]{2,0,1:T(2,128)(2,1)S(1)} %copy.40), channel_id=1, replica_groups=mesh['tm'=8,'strip'=4] {'strip'}, dimensions={1}, use_global_device_ids=true | all-gather | bytes 184320 | tf_op jit(solution)/shard_map/all_gather | solution.py:100
  24.6 135.8 %fusion.96 = f32[128,16,2048]{0,1,2:T(8,128)S(1)} fusion(bf16[2,16,2304]{1,0,2:T(2,128)(2,1)S(1)} %copy.41, bf16[128,2,256]{0,1,2:T(2,128)(2,1)S(1)} %copy.42), kind=kOutput, calls=%fused_computation.124 | convolution fusion | flops 4294967296 | bytes 17055744 | tf_op jit(solution)/shard_map/slice | solution.py:49
  160.4 16.4 %add_convert_fusion = (bf16[64,16,2048]{0,1,2:T(8,128)(2,1)}, bf16[64,16,2048]{0,1,2:T(8,128)(2,1)}) fusion(f32[128,16,2048]{0,1,2:T(8,128)S(1)} %fusion.96, f32[16,2048]{0,1:T(8,128)S(1)} %bitcast.78, f32[16,2048]{0,1:T(8,128)S(1)} %bitcast.77), kind=kLoop, calls=%fused_computation.11 | loop fusion | flops 16777216 | bytes 25427968 | tf_op jit(solution)/shard_map/convert.11
  176.8 12.0 %copy.45 = bf16[64,16,2048]{2,1,0:T(8,128)(2,1)} copy(bf16[64,16,2048]{0,1,2:T(8,128)(2,1)} %get-tuple-element.7) | data formatting | bytes 8388608 | tf_op jit(solution)/shard_map/convert.11
  188.8 12.1 %copy.46 = bf16[64,16,2048]{2,1,0:T(8,128)(2,1)} copy(bf16[64,16,2048]{0,1,2:T(8,128)(2,1)} %get-tuple-element.8) | data formatting | bytes 8388608 | tf_op jit(solution)/shard_map/convert.10
  200.9 7.6 pad_maximum_fusion
  208.5 21.4 %copy.47 = bf16[2,1024,2048]{1,0,2:T(2,128)(2,1)} copy(bf16[2,1024,2048]{2,1,0:T(8,128)(2,1)} %pad_maximum_fusion) | data formatting | bytes 16777216 | tf_op jit(solution)/shard_map/stack | solution.py:53
  235.2 94.0 %all-to-all-done = bf16[2,1024,2048]{1,0,2:T(2,128)(2,1)} async-done(((bf16[2,1024,2048]{1,0,2:T(2,128)(2,1)}), bf16[2,1024,2048]{1,0,2:T(2,128)(2,1)}, u32[]{:S(2)}, u32[]{:S(2)}) %all-to-all-start) | async-done | bytes 8388640 | tf_op jit(solution)/shard_map/all_to_all | solution.py:106
  329.1 17.4 %fusion.94 = (bf16[1,1024,2048]{1,0,2:T(2,128)(2,1)S(1)}, bf16[1,1024,2048]{1,0,2:T(2,128)(2,1)}) fusion(bf16[2,1024,2048]{1,0,2:T(2,128)(2,1)} %all-to-all-done), kind=kLoop, calls=%fused_computation.122 | loop fusion | bytes 16777216 | tf_op jit(solution)/shard_map/slice | solution.py:67
  350.3 6.9 copy.58
  357.2 6.9 fusion.45
  372.3 7.2 copy.59
  379.5 6.9 fusion.47
  386.4 15.8 %fusion.7 = (bf16[1024,8,256]{2,1,0:T(8,128)(2,1)}, bf16[1024,8,256]{2,1,0:T(8,128)(2,1)}) fusion(f32[8,256]{1,0:T(8,128)S(1)} %get-tuple-element.19, f32[8,256]{1,0:T(8,128)S(1)} %get-tuple-element.18, f32[1024,256,8]{1,2,0:T(8,128)} %fusion.45, f32[1024,256,8]{1,2,0:T(8,128)} %fusion.51, f32[1024,256,8]{1,2,0:T(8,128)} %fusion.47, ...), kind=kOutput, calls=%fused_computation.19 | convolution fusion | flops 54526976 | bytes 37765120 | tf_op jit(solution)/shard_map/qn,rns->rqs/dot_general | solution.py:69
  402.1 7.4 stack.44
  409.5 20.6 %copy.50 = bf16[1,1024,2048]{1,0,2:T(2,128)(2,1)} copy(bf16[1,1024,2048]{2,1,0:T(8,128)(2,1)} %stack.44) | data formatting | bytes 8388608 | tf_op jit(solution)/shard_map/stack | solution.py:76
  430.0 7.4 stack.45
  437.4 20.3 %copy.51 = bf16[1,1024,2048]{1,0,2:T(2,128)(2,1)} copy(bf16[1,1024,2048]{2,1,0:T(8,128)(2,1)} %stack.45) | data formatting | bytes 8388608 | tf_op jit(solution)/shard_map/stack | solution.py:76
  457.7 19.7 %pad_maximum_fusion.1 = bf16[2,1024,2048]{1,0,2:T(2,128)(2,1)} fusion(bf16[1,1024,2048]{1,0,2:T(2,128)(2,1)} %copy.51, bf16[1,1024,2048]{1,0,2:T(2,128)(2,1)} %copy.50), kind=kLoop, calls=%fused_computation.14 | loop fusion | flops 16777216 | bytes 16777216 | tf_op jit(solution)/shard_map/stack | solution.py:76
  477.4 5.2 all-to-all-start.1
  482.6 62.8 %multiply_convert_fusion.22 = bf16[2048,2048]{1,0:T(8,128)(2,1)} fusion(), kind=kLoop, calls=%fused_computation.7.clone.1.clone | loop fusion | flops 67108864 | bytes 8388608 | tf_op jit(solution)/shard_map/dot_general | solution.py:86
  545.4 63.3 %multiply_convert_fusion.20 = bf16[2048,2048]{1,0:T(8,128)(2,1)} fusion(), kind=kLoop, calls=%fused_computation.6.clone.1.clone.clone.clone.1 | loop fusion | flops 67108864 | bytes 8388608 | tf_op jit(solution)/shard_map/dot_general | solution.py:86
  608.7 62.8 %multiply_convert_fusion.21 = bf16[2048,2048]{1,0:T(8,128)(2,1)} fusion(), kind=kLoop, calls=%fused_computation.7.clone.clone.1 | loop fusion | flops 67108864 | bytes 8388608 | tf_op jit(solution)/shard_map/dot_general | solution.py:89
  671.5 63.3 %multiply_convert_fusion.19 = bf16[2048,2048]{1,0:T(8,128)(2,1)} fusion(), kind=kLoop, calls=%fused_computation.6.clone.clone.clone.clone.1 | loop fusion | flops 67108864 | bytes 8388608 | tf_op jit(solution)/shard_map/dot_general | solution.py:89
  734.8 17.6 %fusion.93 = (bf16[1,1024,2048]{1,0,2:T(2,128)(2,1)}, bf16[1,1024,2048]{1,0,2:T(2,128)(2,1)}) fusion(bf16[2,1024,2048]{1,0,2:T(2,128)(2,1)} %all-to-all-done.1), kind=kLoop, calls=%fused_computation.121 | loop fusion | bytes 16777216 | tf_op jit(solution)/shard_map/slice | solution.py:86
  752.4 20.1 %copy.62 = bf16[1,1024,2048]{2,1,0:T(8,128)(2,1)} copy(bf16[1,1024,2048]{1,0,2:T(2,128)(2,1)} %get-tuple-element.9) | data formatting | bytes 8388608
  772.5 19.8 %copy.63 = bf16[1,1024,2048]{2,1,0:T(8,128)(2,1)} copy(bf16[1,1024,2048]{1,0,2:T(2,128)(2,1)} %get-tuple-element.10) | data formatting | bytes 8388608
  792.3 14.9 %fusion.11 = f32[1024,2048]{1,0:T(8,128)} fusion(bf16[1,1024,2048]{2,1,0:T(8,128)(2,1)} %copy.62, bf16[2048,2048]{1,0:T(8,128)(2,1)} %multiply_convert_fusion.22), kind=kOutput, calls=%fused_computation.27 | convolution fusion | flops 8589934592 | bytes 20971520 | tf_op jit(solution)/shard_map/dot_general | solution.py:86
  807.2 13.3 %fusion.10 = f32[1024,2048]{1,0:T(8,128)} fusion(bf16[1,1024,2048]{2,1,0:T(8,128)(2,1)S(1)} %copy-done.2, bf16[2048,2048]{1,0:T(8,128)(2,1)} %multiply_convert_fusion.21), kind=kOutput, calls=%fused_computation.26 | convolution fusion | flops 8589934592 | bytes 20971520 | tf_op jit(solution)/shard_map/dot_general | solution.py:89
  820.5 12.1 %add_convert_fusion.1 = bf16[1024,2048]{1,0:T(8,128)(2,1)} fusion(f32[1024,2048]{1,0:T(8,128)} %fusion.11, bf16[1,1024,2048]{2,1,0:T(8,128)(2,1)S(1)} %copy-done.2, bf16[2048,2048]{1,0:T(8,128)(2,1)S(1)} %bitcast.76), kind=kOutput, calls=%fused_computation.25 | convolution fusion | flops 8594128896 | bytes 25165824 | tf_op jit(solution)/shard_map/dot_general | solution.py:86
  832.7 12.1 %subtract_convert_fusion.1 = bf16[1024,2048]{1,0:T(8,128)(2,1)} fusion(f32[1024,2048]{1,0:T(8,128)} %fusion.10, bf16[1,1024,2048]{2,1,0:T(8,128)(2,1)S(1)} %copy-done.1, bf16[2048,2048]{1,0:T(8,128)(2,1)S(1)} %bitcast.74), kind=kOutput, calls=%fused_computation.24 | convolution fusion | flops 8594128896 | bytes 25165824 | tf_op jit(solution)/shard_map/dot_general | solution.py:89
  844.9 6.3 pad_maximum_fusion.2
  (49 shorter events, 26.3 us)
Async XLA Ops:
  0.7 3.0 collective-permute-start
  24.6 135.8 %copy-start.3 = (f32[1,16,2048]{1,2,0:T(8,128)S(1)}, f32[1,16,2048]{1,2,0:T(8,128)}, u32[]{:S(2)}) copy-start(f32[1,16,2048]{1,2,0:T(8,128)} %copy.56) | copy-start | bytes 393220
  24.6 135.8 %copy-start.4 = (f32[1,16,2048]{1,2,0:T(8,128)S(1)}, f32[1,16,2048]{1,2,0:T(8,128)}, u32[]{:S(2)}) copy-start(f32[1,16,2048]{1,2,0:T(8,128)} %copy.57) | copy-start | bytes 393220
  229.9 99.2 %all-to-all-start = ((bf16[2,1024,2048]{1,0,2:T(2,128)(2,1)}), bf16[2,1024,2048]{1,0,2:T(2,128)(2,1)}, u32[]{:S(2)}, u32[]{:S(2)}) async-start(bf16[2,1024,2048]{1,0,2:T(2,128)(2,1)} %copy.47), calls=%async_computation | async-start | bytes 16777216 | tf_op jit(solution)/shard_map/all_to_all | solution.py:106
  357.2 6.9 copy-start
  357.2 11.4 %slice-start = ((s8[8388608]{0:T(1024)(128)(4,1)}), s8[4194304]{0:T(1024)(128)(4,1)S(1)}, s32[]{:S(2)}) async-start(s8[8388608]{0:T(1024)(128)(4,1)} %bitcast.67), calls=%async_computation.2 | async-start | bytes 8388608
  364.1 4.5 slice-start.1
  477.4 257.4 %all-to-all-start.1 = ((bf16[2,1024,2048]{1,0,2:T(2,128)(2,1)}), bf16[2,1024,2048]{1,0,2:T(2,128)(2,1)}, u32[]{:S(2)}, u32[]{:S(2)}) async-start(bf16[2,1024,2048]{1,0,2:T(2,128)(2,1)} %pad_maximum_fusion.1), calls=%async_computation.1 | async-start | bytes 16777216 | tf_op jit(solution)/shard_map/all_to_all | solution.py:108
  792.3 14.9 %copy-start.2 = (bf16[1,1024,2048]{2,1,0:T(8,128)(2,1)S(1)}, bf16[1,1024,2048]{2,1,0:T(8,128)(2,1)}, u32[]{:S(2)}) copy-start(bf16[1,1024,2048]{2,1,0:T(8,128)(2,1)} %copy.63) | copy-start | bytes 12582916
  792.3 28.2 %slice-start.4 = ((s8[8388608]{0:T(1024)(128)(4,1)}), s8[4194304]{0:T(1024)(128)(4,1)S(1)}, s32[]{:S(2)}) async-start(s8[8388608]{0:T(1024)(128)(4,1)} %bitcast.75), calls=%async_computation.6 | async-start | bytes 8388608
  792.3 40.4 %slice-start.2 = ((s8[8388608]{0:T(1024)(128)(4,1)}), s8[4194304]{0:T(1024)(128)(4,1)S(1)}, s32[]{:S(2)}) async-start(s8[8388608]{0:T(1024)(128)(4,1)} %bitcast.73), calls=%async_computation.4 | async-start | bytes 8388608
  807.2 13.4 %slice-start.5 = ((s8[8388608]{0:T(1024)(128)(4,1)}), s8[4194304]{0:T(1024)(128)(4,1)S(1)}, s32[]{:S(2)}) async-start(s8[8388608]{0:T(1024)(128)(4,1)} %bitcast.75), calls=%async_computation.7 | async-start | bytes 8388608
  807.2 25.5 %slice-start.3 = ((s8[8388608]{0:T(1024)(128)(4,1)}), s8[4194304]{0:T(1024)(128)(4,1)S(1)}, s32[]{:S(2)}) async-start(s8[8388608]{0:T(1024)(128)(4,1)} %bitcast.73), calls=%async_computation.5 | async-start | bytes 8388608
  820.5 12.2 %copy-start.1 = (bf16[1,1024,2048]{2,1,0:T(8,128)(2,1)S(1)}, bf16[1,1024,2048]{2,1,0:T(8,128)(2,1)}, u32[]{:S(2)}) copy-start(bf16[1,1024,2048]{2,1,0:T(8,128)(2,1)} %copy.62) | copy-start | bytes 12582916
  832.7 12.1 %copy-start.5 = (bf16[1024,2048]{1,0:T(8,128)(2,1)S(1)}, bf16[1024,2048]{1,0:T(8,128)(2,1)}, u32[]{:S(2)}) copy-start(bf16[1024,2048]{1,0:T(8,128)(2,1)} %add_convert_fusion.1) | copy-start | bytes 12582916
where the time goes:
time: 858 us; the launch traced here: 852 us
  other arithmetic  304 us (35%)
  matrix products  222 us (26%)
  local copies, waits for them, and re-layouts  203 us (24%)
  waiting for transfers between devices  95.2 us (11%)
  blocking collectives  15.4 us (2%)
  starting transfers between devices  11.6 us (1%)
    slice x1, matrix products, channelize(): outcome[:, :, :length].reshape(2, channel_count, window_count, length)  136 us
    all_to_all x1, waiting for transfers between devices, per_device(): lax.all_to_all(strips, 'tm', split_axis=2, concat_axis=2, tiled=True)  94 us
    dot_general x1, other arithmetic, second_pass(): jnp.dot(values[0], big_sin, preferred_element_type=jnp.float32)  63.3 us
    dot_general x1, other arithmetic, second_pass(): jnp.dot(values[1], big_sin, preferred_element_type=jnp.float32)  63.3 us
    dot_general x1, other arithmetic, second_pass(): jnp.dot(values[0], big_cos, preferred_element_type=jnp.float32)  62.8 us
    dot_general x1, other arithmetic, second_pass(): jnp.dot(values[1], big_cos, preferred_element_type=jnp.float32)  62.8 us
    another operation x4, local copies, waits for them, and re-layouts, first_pass(): turned = jnp.stack([turned_real, turned_imag]).astype(jnp.bfloat16)  55.5 us
    unnamed x28, local copies, waits for them, and re-layouts  47.4 us
  transfers between devices with their start and end apart: 3, of which 2 were waited for; matrix products, arithmetic and copies ran while one was open for 30% of the time, Pallas kernels for 0%

commit v1 on v0

v1 whole, which is shorter than its diff:
```python
import math

import jax
import jax.numpy as jnp
from jax import lax
from jax.experimental import pallas as pl
from jax.experimental.pallas import tpu as pltpu
from jax.sharding import PartitionSpec as P

K = 256
D = 8
EXTRA = 16
TWO_PI = 2.0 * math.pi


def unit_pair(phases, modulus):
    angles = jnp.float32(TWO_PI / modulus) * (phases % modulus).astype(jnp.float32)
    return jnp.cos(angles), jnp.sin(angles)


def channel_filters(channel_ids):
    offsets = jnp.arange(K, dtype=jnp.int32)
    cosine, sine = unit_pair(channel_ids[:, None] * offsets[None, :], K)
    hamming = 0.54 - 0.46 * jnp.cos(jnp.float32(TWO_PI) * offsets.astype(jnp.float32) / K)
    scaled = hamming[None, :] / math.sqrt(K)
    cosine = (scaled * cosine).astype(jnp.bfloat16)
    sine = (scaled * sine).astype(jnp.bfloat16)
    rows = []
    for real_taps, imag_taps in ((cosine, sine), (-sine, cosine)):
        for offset in range(D):
            pad = ((0, 0), (offset, EXTRA - offset))
            rows.append(
                jnp.concatenate([jnp.pad(real_taps, pad), jnp.pad(imag_taps, pad)], axis=1)
            )
    return jnp.concatenate(rows, axis=0)


def small_dft(values):
    count = len(values)
    if count == 1:
        return values
    even = small_dft(values[0::2])
    odd = small_dft(values[1::2])
    low, high = [], []
    for i in range(count // 2):
        er, ei = even[i]
        orr, oi = odd[i]
        if i == 0:
            tr, ti = orr, oi
        elif 4 * i == count:
            tr, ti = oi, -orr
        else:
            c = math.cos(TWO_PI * i / count)
            s = math.sin(TWO_PI * i / count)
            if abs(c - s) < 1e-6:
                tr, ti = (orr + oi) * c, (oi - orr) * c
            elif abs(c + s) < 1e-6:
                tr, ti = (oi - orr) * s, (orr + oi) * (-s)
            else:
                tr, ti = orr * c + oi * s, oi * c - orr * s
        low.append((er + tr, ei + ti))
        high.append((er - tr, ei - ti))
    return low + high


def make_body(blocks, piece, chan):
    total = blocks * piece
    rows = D * chan

    def body(x_ref, filt_ref, turn_ref, dft_ref, twid_ref, out_ref, taps_ref, acc_ref):
        parts = [x_ref[0, a, 0] for a in range(blocks)]
        parts.append(jnp.zeros((2 * D, 128), jnp.bfloat16))
        x = jnp.concatenate(parts, axis=1).astype(jnp.float32)
        width = total + 128
        span = K + EXTRA
        for c in range(2):
            base = x[c * D : (c + 1) * D]
            for q in range(0, span // D, 2):
                pair = []
                for s in (q, q + 1):
                    moved = base if s == 0 else pltpu.roll(base, width - s, 1)
                    pair.append(moved[:, :total])
                taps_ref[c * span + q * D : c * span + (q + 2) * D, :] = jnp.concatenate(
                    pair, axis=0
                ).astype(jnp.bfloat16)
        lag = K // 2 // D
        xr = pltpu.roll(x[:D], width - lag, 1)[:, :total]
        xi = pltpu.roll(x[D:], width - lag, 1)[:, :total]
        tc, ts = turn_ref[0], turn_ref[1]
        zr = xr * tc - xi * ts
        zi = -(xi * tc + xr * ts)
        for a in range(blocks):
            lanes = slice(a * piece, (a + 1) * piece)
            res = jnp.dot(
                filt_ref[...], taps_ref[:, lanes], preferred_element_type=jnp.float32
            )
            for o in range(D):
                r0 = o * chan
                fr = res[r0 : r0 + chan]
                fi = res[rows + r0 : rows + r0 + chan]
                br = zr[o : o + 1, lanes]
                bi = zi[o : o + 1, lanes]
                pr = fr * br - fi * bi
                pi = fr * bi + fi * br
                if a > 0:
                    pr = pr + acc_ref[r0 : r0 + chan]
                    pi = pi + acc_ref[rows + r0 : rows + r0 + chan]
                acc_ref[r0 : r0 + chan] = pr
                acc_ref[rows + r0 : rows + r0 + chan] = pi
        partial = jnp.concatenate(
            [acc_ref[:rows].astype(jnp.bfloat16), acc_ref[rows:].astype(jnp.bfloat16)], axis=1
        )
        inner = jnp.dot(partial, dft_ref[...], preferred_element_type=jnp.float32)
        turned = []
        for o in range(D):
            vr = inner[o * chan : (o + 1) * chan, :piece]
            vi = inner[o * chan : (o + 1) * chan, piece:]
            if o > 0:
                tc = twid_ref[0, o : o + 1]
                ts = twid_ref[1, o : o + 1]
                vr, vi = vr * tc + vi * ts, vi * tc - vr * ts
            turned.append((vr, vi))
        for m, (yr, yi) in enumerate(small_dft(turned)):
            out_ref[0, 0, :, m * piece : (m + 1) * piece] = yr.astype(jnp.bfloat16)
            out_ref[0, 1, :, m * piece : (m + 1) * piece] = yi.astype(jnp.bfloat16)

    return body


def per_device(signal):
    blocks = lax.axis_size("tm")
    strips = lax.axis_size("strip")
    wloc, block_len = signal.shape[1], signal.shape[2]
    windows = wloc * strips
    piece = block_len // D
    chan = K // strips
    total = block_len * blocks
    span = K + EXTRA
    local = signal.reshape(2, wloc, piece, D).transpose(1, 0, 3, 2).reshape(wloc, 2 * D, piece)
    every = lax.all_gather(local, ("strip", "tm"), axis=0, tiled=False)
    every = every.reshape(strips, blocks, wloc, 2 * D, piece)
    channel_ids = lax.axis_index("strip") * chan + jnp.arange(chan, dtype=jnp.int32)
    filters = channel_filters(channel_ids)
    residue = lax.axis_index("tm")
    offs = jnp.arange(D, dtype=jnp.int32)
    samples = offs[:, None] + D * jnp.arange(piece * blocks, dtype=jnp.int32)[None, :]
    turn = jnp.stack(unit_pair(residue * samples, total)) * (1.0 / math.sqrt(blocks))
    ids = jnp.arange(piece, dtype=jnp.int32)
    dc, ds = unit_pair(ids[:, None] * ids[None, :], piece)
    dft = jnp.concatenate(
        [jnp.concatenate([dc, -ds], axis=1), jnp.concatenate([ds, dc], axis=1)], axis=0
    ) * (1.0 / math.sqrt(block_len))
    dft = dft.astype(jnp.bfloat16)
    twid = jnp.stack(unit_pair(offs[:, None] * ids[None, :], block_len))

    fixed = lambda *dims: pl.BlockSpec(dims, lambda w: (0,) * len(dims))
    out = pl.pallas_call(
        make_body(blocks, piece, chan),
        grid=(windows,),
        in_specs=[
            pl.BlockSpec((1, blocks, 1, 2 * D, piece), lambda w: (w // wloc, 0, w % wloc, 0, 0)),
            fixed(2 * D * chan, 2 * span),
            fixed(2, D, piece * blocks),
            fixed(2 * piece, 2 * piece),
            fixed(2, D, piece),
        ],
        out_specs=pl.BlockSpec((1, 2, chan, block_len), lambda w: (w, 0, 0, 0)),
        out_shape=jax.ShapeDtypeStruct((windows, 2, chan, block_len), jnp.bfloat16),
        scratch_shapes=[
            pltpu.VMEM((2 * span, piece * blocks), jnp.bfloat16),
            pltpu.VMEM((2 * D * chan, piece), jnp.float32),
        ],
        compiler_params=pltpu.CompilerParams(
            dimension_semantics=("arbitrary",), vmem_limit_bytes=56 * 1024 * 1024
        ),
        name="strip_windows",
    )(every, filters, turn, dft, twid)
    return out.transpose(1, 2, 0, 3).reshape(2, chan, windows, 1, block_len)


def solution(mesh):
    return jax.shard_map(
        per_device,
        mesh=mesh,
        in_specs=(P(None, "strip", "tm"),),
        out_specs=P(None, "strip", None, "tm", None),
        check_vma=False,
    )
```

time: 858 us -> 165 us (0.19)
  other arithmetic: 304 us -> 6.72 us
  matrix products: 222 us -> 0 us
  local copies, waits for them, and re-layouts: 203 us -> 13.7 us
  Pallas kernels: 0 us -> 79.5 us
  waiting for transfers between devices: 95.2 us -> 50.8 us
  blocking collectives: 15.4 us -> 0 us
  between operations: 0.71 us -> 13.5 us
  starting transfers between devices: 11.6 us -> 0.01 us
    dot_general x4 -> x0, other arithmetic: 252 us -> none  [the longest x1 63.3 us: second_pass(): jnp.dot(values[0], big_sin, preferred_element_type=jnp.float32)]
    slice x1 -> x0, matrix products: 136 us -> none  [channelize(): outcome[:, :, :length].reshape(2, channel_count, window_count, length)]
    another operation x7 -> x0, local copies, waits for them, and re-layouts: 101 us -> none  [the longest x4 55.5 us: first_pass(): turned = jnp.stack([turned_real, turned_imag]).astype(jnp.bfloat16)]
    all_to_all x2 -> x0, waiting for transfers between devices: 94 us -> none  [the longest x1 94 us: per_device(): lax.all_to_all(strips, 'tm', split_axis=2, concat_axis=2, tiled=True)]
    dot_general x8 -> x0, matrix products: 86.5 us -> none  [the longest x1 15.8 us: first_pass(): jnp.einsum('qn,rns->rqs', small_cos, grouped[1], preferred_element_type=j...]
    pallas_call x0 -> x1, Pallas kernels: none -> 79.5 us  [per_device(): pl.pallas_call(make_body(blocks, piece, chan), grid=(windows,), in_specs=...]
    all_gather x0 -> x1, waiting for transfers between devices: none -> 50.8 us  [per_device(): every = lax.all_gather(local, ('strip', 'tm'), axis=0, tiled=False)]
    another operation x5 -> x1, other arithmetic: 50.4 us -> 0.6 us  [per_device(): twid = jnp.stack(unit_pair(offs[:, None] * ids[None, :], block_len))]
  transfers between devices with their start and end apart: 3 -> 1, of which waited for: 2 -> 1; matrix products, arithmetic and copies ran while one was open for 30% -> 4% of each run, Pallas kernels for 0% -> 0%
where the time goes in v1:
time: 165 us; the launch traced here: 164 us
  Pallas kernels  79.5 us (48%)
  waiting for transfers between devices  50.8 us (31%)
  local copies, waits for them, and re-layouts  13.7 us (8%)
  between operations  13.5 us (8%)
  other arithmetic  6.72 us (4%)
    pallas_call x1, Pallas kernels, per_device(): pl.pallas_call(make_body(blocks, piece, chan), grid=(windows,), in_specs=...  79.5 us
    all_gather x1, waiting for transfers between devices, per_device(): every = lax.all_gather(local, ('strip', 'tm'), axis=0, tiled=False)  50.8 us
    reshape x1, local copies, waits for them, and re-layouts, per_device(): return out.transpose(1, 2, 0, 3).reshape(2, chan, windows, 1, block_len)  11.4 us
  transfers between devices with their start and end apart: 1, of which 1 were waited for; matrix products, arithmetic and copies ran while one was open for 4% of the time, Pallas kernels for 0%

profile of v1, /device:TPU:0, one launch (start us, length us, event | category | flops | bytes accessed | tf_op | source)
XLA Modules:
  0.0 164.3 jit_solution(9817998009693379104)
XLA Ops:
  6.5 1.4 reshape.198
  7.9 0.8 copy.7
  8.7 0.0 all-gather.2.cloned.1.call-update
  8.8 0.1 fusion.75
  8.9 0.3 fusion.77
  9.2 0.3 multiply_convert_fusion.1
  9.6 0.2 fusion.78
  9.7 0.6 pad_maximum_fusion.twid_ref
  10.3 0.1 fusion.27
  10.4 0.1 fusion.29
  10.5 0.1 fusion.31
  10.6 0.1 fusion.33
  10.7 0.1 fusion.35
  10.8 0.1 fusion.37
  10.9 0.1 fusion.39
  11.0 0.1 fusion.41
  11.1 0.1 fusion.43
  11.2 0.1 fusion.45
  11.3 0.1 fusion.47
  11.4 0.1 fusion.49
  11.5 0.1 fusion.51
  11.6 0.1 fusion.53
  11.7 0.1 fusion.55
  11.8 0.1 fusion.57.filt_ref
  11.9 1.0 fusion.25
  12.9 1.0 fusion.23
  14.0 0.9 fusion.dft_ref
  14.8 0.3 fusion.68
  15.1 0.7 maximum_multiply_fusion.1.turn_ref
  15.8 50.8 %all-gather.2.cloned.1.call-done = bf16[32,4,16,256]{3,2,1,0:T(8,128)(2,1)} async-done(((bf16[1,4,16,256]{3,2,1,0:T(8,128)(2,1)}), bf16[32,4,16,256]{3,2,1,0:T(8,128)(2,1)}) %all-gather.2.cloned.1.call-update) | async-done | bytes 1048592 | tf_op jit(solution)/shard_map/all_gather | solution.py:140
  66.6 79.5 %strip_windows.1 = bf16[16,2,64,2048]{3,2,1,0:T(8,128)(2,1)} custom-call(bf16[4,8,4,16,256]{4,3,2,1,0:T(8,128)(2,1)} %bitcast.8, bf16[1024,544]{1,0:T(8,128)(2,1)} %copy-done, f32[2,8,2048]{2,1,0:T(8,128)} %maximum_multiply_fusion.1.turn_ref, bf16[512,512]{1,0:T(8,128)(2,1)} %fusion.dft_ref, f32[2,8,256]{2,1,0:T(8,128)} %pad_maximum_fusion.twid_ref), custom_call_target="tpu_custom_call" | custom-call | tf_op jit(solution)/shard_map/strip_windows/pallas_call | solution.py:157
  146.0 11.4 %copy.8 = bf16[2,64,16,1,2048]{4,2,3,1,0:T(8,128)(2,1)} copy(bf16[2,64,16,1,2048]{4,1,0,2,3:T(8,128)(2,1)} %bitcast.6) | data formatting | bytes 16777216 | tf_op jit(solution)/shard_map/reshape | solution.py:178
  (6 shorter events, 0.1 us)
Async XLA Ops:
  6.5 60.0 %all-gather.2.cloned.1.call-start = ((), (), s32[]{:S(2)}) async-start(), calls=%async_computation | async-start | bytes 1081344 | tf_op jit(solution)/shard_map/all_gather | solution.py:140
  11.9 54.6 %copy-start = (bf16[1024,544]{1,0:T(8,128)(2,1)}, bf16[1024,544]{1,0:T(8,128)(2,1)S(1)}, u32[]{:S(2)}) copy-start(bf16[1024,544]{1,0:T(8,128)(2,1)S(1)} %fusion.57.filt_ref) | copy-start | bytes 3342340
Sparse Core Ops, SparseCore 0:
  10.2 56.3 all-gather.1
